TPU v7x, 32 devices: a whole 2x2x4 slice. The times are simulated.
32 devices in a mesh: tm: 8 (over z, x), col: 4 (over y, core).
Axes of the slice: x: 2, y: 2, z: 4, core: 2. Of those that a mesh axis runs over, the one named last changes fastest.
Arguments:
- jacobians: float32 [96, 512, 512], P('tm'), may hold values from -0.05 to 1.05
- increments: float32 [96, 512], P('tm'), may hold values from -1.5 to 1.5
- initial: float32 [512], P('col'), may hold values from -6 to 6
Outputs:
- states: float32 [96, 512], P('tm', 'col')
All inputs are finite; a program needn't handle non-finite values.
Results may differ from a plain program's by a relative error of at most 0.0003.
Values sent between devices are 32-bit elements; how exact they have to be, the bound alone decides.
No kernel may reach another device: no remote copies, remote signals or barrier semaphores. Data moves between devices by JAX's collectives and lax.ppermute only.
A program may use at most 128 MiB of HBM per device.

v0:
```python
import jax
import jax.numpy as jnp
from jax import lax
from jax.sharding import PartitionSpec as P


def from_behind(block, axis, distance):
    devices = range(lax.axis_size(axis))
    route = [(i - distance, i) for i in devices if i - distance in devices]
    return lax.ppermute(block, axis, route)


def matmul(left, right):
    return jnp.dot(left, right, precision=lax.Precision.HIGHEST, preferred_element_type=jnp.float32)


def body(jacobians, increments, initial):
    part_cols = initial.shape[0]
    column_index = lax.axis_index("col")
    segment_index = lax.axis_index("tm")
    rounds = (lax.axis_size("tm") - 1).bit_length()
    first_col = column_index * part_cols

    def own_cols(matrix):
        return lax.dynamic_slice_in_dim(matrix, first_col, part_cols, matrix.ndim - 1)

    def advance_map(running, inputs):
        step_jac, step_inc = inputs
        return ((matmul(step_jac, running[0]), matmul(step_jac, running[1]) + step_inc), None)

    composed, _ = lax.scan(
        advance_map, (own_cols(jacobians[0]), increments[0]), (jacobians[1:], increments[1:])
    )
    acc_map, acc_off = composed
    for level_index in range(rounds):
        distance = 1 << level_index
        recv_map, recv_off = from_behind((acc_map, acc_off), "tm", distance)

        def fold_columns(running, col_block, first_row, recv_map=recv_map, recv_off=recv_off):
            return (matmul(col_block, recv_map), running[1] + matmul(col_block, recv_off))

        new_map, new_off = fold_columns(
            (jnp.zeros_like(acc_map), acc_off),
            lax.all_gather(acc_map, "col", axis=1, tiled=True),
            jnp.int32(0),
        )
        active = segment_index >= distance
        acc_map = jnp.where(active, new_map, acc_map)
        acc_off = jnp.where(active, new_off, acc_off)
    end_part = matmul(acc_map, initial)
    end_mine = lax.psum_scatter(end_part, "col", scatter_dimension=0, tiled=True) + own_cols(
        acc_off
    )
    handed = from_behind(end_mine, "tm", 1)
    start_mine = jnp.where(segment_index == 0, initial, handed)
    start_full = lax.all_gather(start_mine, "col", axis=0, tiled=True)

    def advance_state(current, inputs):
        step_jac, step_inc = inputs
        following = matmul(step_jac, current) + step_inc
        return (following, own_cols(following))

    _, leading = lax.scan(advance_state, start_full, (jacobians[:-1], increments[:-1]))
    return jnp.concatenate([leading, end_mine[None, :]], axis=0)


def solution(mesh):
    return jax.shard_map(
        body,
        mesh=mesh,
        in_specs=(P("tm", None, None), P("tm", None), P("col")),
        out_specs=P("tm", "col"),
        check_vma=False,
    )
```

profile of v0, /device:TPU:25, one launch (start us, length us, event | category | flops | bytes accessed | tf_op | source)
XLA Modules:
  0.0 202.7 jit_solution(5260583161376502509)
XLA Ops:
  6.5 17.6 %fusion.15 = (f32[11,512,512]{2,1,0:T(8,128)}, f32[11,512,512]{2,1,0:T(8,128)}) fusion(f32[12,512,512]{2,1,0:T(8,128)} %param.7), kind=kLoop, calls=%fused_computation.28 | loop fusion | bytes 46137344 | tf_op jit(solution)/shard_map/slice | solution.py:63
  24.2 49.5 %while.26 = (s32[]{:T(128)}, f32[512,128]{1,0:T(8,128)S(1)}, f32[512]{0:T(512)S(1)}, f32[11,512,512]{2,1,0:T(8,128)}, f32[11,512]{1,0:T(8,128)S(1)}, /*index=5*/s32[]{:T(128)}) while((s32[]{:T(128)}, f32[512,128]{1,0:T(8,128)S(1)}, f32[512]{0:T(512)S(1)}, f32[11,512,512]{2,1,0:T(8,128)}, f32[11,512]{1,0:T(8,128)S(1)}, ...), condition=%wide.region_1.2_spmd, body=%wide.region_0.1_spmd.sunk | while | flops 405799424 | bytes 3161161 | solution.py:31
  24.2 2.2 %fusion.50 = f32[1,512]{1,0:T(1,128)S(1)} fusion(f32[512,1]{0,1:T(1,128)S(1)} %bitcast.80, f32[11,512,512]{2,1,0:T(8,128)} %get-tuple-element.219, s32[]{:T(128)} %get-tuple-element.210), kind=kOutput, calls=%fused_computation.clone.1 | convolution fusion | flops 3145728 | bytes 1053184 | tf_op jit(solution)/shard_map/while/body/eval_jaxpr/dot_general | solution.py:14
  26.5 2.2 %fusion.49 = f32[512,128]{1,0:T(8,128)S(1)} fusion(f32[512,128]{1,0:T(8,128)S(1)} %copy.24, f32[11,512,512]{2,1,0:T(8,128)} %get-tuple-element.219, s32[]{:T(128)} %get-tuple-element.210), kind=kOutput, calls=%fused_computation.2.clone.1 | convolution fusion | flops 402653184 | bytes 1573376 | tf_op jit(solution)/shard_map/while/body/eval_jaxpr/dot_general | solution.py:14
  28.7 2.2 %fusion.50 = f32[1,512]{1,0:T(1,128)S(1)} fusion(f32[512,1]{0,1:T(1,128)S(1)} %bitcast.80, f32[11,512,512]{2,1,0:T(8,128)} %get-tuple-element.219, s32[]{:T(128)} %get-tuple-element.210), kind=kOutput, calls=%fused_computation.clone.1 | convolution fusion | flops 3145728 | bytes 1053184 | tf_op jit(solution)/shard_map/while/body/eval_jaxpr/dot_general | solution.py:14
  31.0 2.2 %fusion.49 = f32[512,128]{1,0:T(8,128)S(1)} fusion(f32[512,128]{1,0:T(8,128)S(1)} %copy.24, f32[11,512,512]{2,1,0:T(8,128)} %get-tuple-element.219, s32[]{:T(128)} %get-tuple-element.210), kind=kOutput, calls=%fused_computation.2.clone.1 | convolution fusion | flops 402653184 | bytes 1573376 | tf_op jit(solution)/shard_map/while/body/eval_jaxpr/dot_general | solution.py:14
  33.2 2.2 %fusion.50 = f32[1,512]{1,0:T(1,128)S(1)} fusion(f32[512,1]{0,1:T(1,128)S(1)} %bitcast.80, f32[11,512,512]{2,1,0:T(8,128)} %get-tuple-element.219, s32[]{:T(128)} %get-tuple-element.210), kind=kOutput, calls=%fused_computation.clone.1 | convolution fusion | flops 3145728 | bytes 1053184 | tf_op jit(solution)/shard_map/while/body/eval_jaxpr/dot_general | solution.py:14
  35.5 2.2 %fusion.49 = f32[512,128]{1,0:T(8,128)S(1)} fusion(f32[512,128]{1,0:T(8,128)S(1)} %copy.24, f32[11,512,512]{2,1,0:T(8,128)} %get-tuple-element.219, s32[]{:T(128)} %get-tuple-element.210), kind=kOutput, calls=%fused_computation.2.clone.1 | convolution fusion | flops 402653184 | bytes 1573376 | tf_op jit(solution)/shard_map/while/body/eval_jaxpr/dot_general | solution.py:14
  40.0 2.2 %fusion.49 = f32[512,128]{1,0:T(8,128)S(1)} fusion(f32[512,128]{1,0:T(8,128)S(1)} %copy.24, f32[11,512,512]{2,1,0:T(8,128)} %get-tuple-element.219, s32[]{:T(128)} %get-tuple-element.210), kind=kOutput, calls=%fused_computation.2.clone.1 | convolution fusion | flops 402653184 | bytes 1573376 | tf_op jit(solution)/shard_map/while/body/eval_jaxpr/dot_general | solution.py:14
  42.2 2.2 %fusion.50 = f32[1,512]{1,0:T(1,128)S(1)} fusion(f32[512,1]{0,1:T(1,128)S(1)} %bitcast.80, f32[11,512,512]{2,1,0:T(8,128)} %get-tuple-element.219, s32[]{:T(128)} %get-tuple-element.210), kind=kOutput, calls=%fused_computation.clone.1 | convolution fusion | flops 3145728 | bytes 1053184 | tf_op jit(solution)/shard_map/while/body/eval_jaxpr/dot_general | solution.py:14
  44.5 2.2 %fusion.49 = f32[512,128]{1,0:T(8,128)S(1)} fusion(f32[512,128]{1,0:T(8,128)S(1)} %copy.24, f32[11,512,512]{2,1,0:T(8,128)} %get-tuple-element.219, s32[]{:T(128)} %get-tuple-element.210), kind=kOutput, calls=%fused_computation.2.clone.1 | convolution fusion | flops 402653184 | bytes 1573376 | tf_op jit(solution)/shard_map/while/body/eval_jaxpr/dot_general | solution.py:14
  46.7 2.2 %fusion.50 = f32[1,512]{1,0:T(1,128)S(1)} fusion(f32[512,1]{0,1:T(1,128)S(1)} %bitcast.80, f32[11,512,512]{2,1,0:T(8,128)} %get-tuple-element.219, s32[]{:T(128)} %get-tuple-element.210), kind=kOutput, calls=%fused_computation.clone.1 | convolution fusion | flops 3145728 | bytes 1053184 | tf_op jit(solution)/shard_map/while/body/eval_jaxpr/dot_general | solution.py:14
  49.0 2.2 %fusion.49 = f32[512,128]{1,0:T(8,128)S(1)} fusion(f32[512,128]{1,0:T(8,128)S(1)} %copy.24, f32[11,512,512]{2,1,0:T(8,128)} %get-tuple-element.219, s32[]{:T(128)} %get-tuple-element.210), kind=kOutput, calls=%fused_computation.2.clone.1 | convolution fusion | flops 402653184 | bytes 1573376 | tf_op jit(solution)/shard_map/while/body/eval_jaxpr/dot_general | solution.py:14
  53.5 2.2 %fusion.49 = f32[512,128]{1,0:T(8,128)S(1)} fusion(f32[512,128]{1,0:T(8,128)S(1)} %copy.24, f32[11,512,512]{2,1,0:T(8,128)} %get-tuple-element.219, s32[]{:T(128)} %get-tuple-element.210), kind=kOutput, calls=%fused_computation.2.clone.1 | convolution fusion | flops 402653184 | bytes 1573376 | tf_op jit(solution)/shard_map/while/body/eval_jaxpr/dot_general | solution.py:14
  55.7 2.2 %fusion.50 = f32[1,512]{1,0:T(1,128)S(1)} fusion(f32[512,1]{0,1:T(1,128)S(1)} %bitcast.80, f32[11,512,512]{2,1,0:T(8,128)} %get-tuple-element.219, s32[]{:T(128)} %get-tuple-element.210), kind=kOutput, calls=%fused_computation.clone.1 | convolution fusion | flops 3145728 | bytes 1053184 | tf_op jit(solution)/shard_map/while/body/eval_jaxpr/dot_general | solution.py:14
  58.0 2.2 %fusion.49 = f32[512,128]{1,0:T(8,128)S(1)} fusion(f32[512,128]{1,0:T(8,128)S(1)} %copy.24, f32[11,512,512]{2,1,0:T(8,128)} %get-tuple-element.219, s32[]{:T(128)} %get-tuple-element.210), kind=kOutput, calls=%fused_computation.2.clone.1 | convolution fusion | flops 402653184 | bytes 1573376 | tf_op jit(solution)/shard_map/while/body/eval_jaxpr/dot_general | solution.py:14
  60.2 2.2 %fusion.50 = f32[1,512]{1,0:T(1,128)S(1)} fusion(f32[512,1]{0,1:T(1,128)S(1)} %bitcast.80, f32[11,512,512]{2,1,0:T(8,128)} %get-tuple-element.219, s32[]{:T(128)} %get-tuple-element.210), kind=kOutput, calls=%fused_computation.clone.1 | convolution fusion | flops 3145728 | bytes 1053184 | tf_op jit(solution)/shard_map/while/body/eval_jaxpr/dot_general | solution.py:14
  62.5 2.2 %fusion.49 = f32[512,128]{1,0:T(8,128)S(1)} fusion(f32[512,128]{1,0:T(8,128)S(1)} %copy.24, f32[11,512,512]{2,1,0:T(8,128)} %get-tuple-element.219, s32[]{:T(128)} %get-tuple-element.210), kind=kOutput, calls=%fused_computation.2.clone.1 | convolution fusion | flops 402653184 | bytes 1573376 | tf_op jit(solution)/shard_map/while/body/eval_jaxpr/dot_general | solution.py:14
  67.0 2.2 %fusion.49 = f32[512,128]{1,0:T(8,128)S(1)} fusion(f32[512,128]{1,0:T(8,128)S(1)} %copy.24, f32[11,512,512]{2,1,0:T(8,128)} %get-tuple-element.219, s32[]{:T(128)} %get-tuple-element.210), kind=kOutput, calls=%fused_computation.2.clone.1 | convolution fusion | flops 402653184 | bytes 1573376 | tf_op jit(solution)/shard_map/while/body/eval_jaxpr/dot_general | solution.py:14
  69.2 2.2 %fusion.50 = f32[1,512]{1,0:T(1,128)S(1)} fusion(f32[512,1]{0,1:T(1,128)S(1)} %bitcast.80, f32[11,512,512]{2,1,0:T(8,128)} %get-tuple-element.219, s32[]{:T(128)} %get-tuple-element.210), kind=kOutput, calls=%fused_computation.clone.1 | convolution fusion | flops 3145728 | bytes 1053184 | tf_op jit(solution)/shard_map/while/body/eval_jaxpr/dot_general | solution.py:14
  71.5 2.2 %fusion.49 = f32[512,128]{1,0:T(8,128)S(1)} fusion(f32[512,128]{1,0:T(8,128)S(1)} %copy.24, f32[11,512,512]{2,1,0:T(8,128)} %get-tuple-element.219, s32[]{:T(128)} %get-tuple-element.210), kind=kOutput, calls=%fused_computation.2.clone.1 | convolution fusion | flops 402653184 | bytes 1573376 | tf_op jit(solution)/shard_map/while/body/eval_jaxpr/dot_general | solution.py:14
  74.5 3.1 %collective-permute-start = (f32[512,128]{1,0:T(8,128)}, f32[512,128]{1,0:T(8,128)S(1)}, u32[]{:S(2)}, u32[]{:S(2)}) collective-permute-start(f32[512,128]{1,0:T(8,128)} %copy-done), channel_id=1, source_target_pairs={{0,4},{4,8},{8,12},{12,16},{16,20},{20,24},{24,28},{1,5},{5,9},{9,... | collective-permute-start | bytes 786440 | tf_op jit(solution)/shard_map/ppermute | solution.py:10
  77.7 7.1 %collective-permute-done = f32[512,128]{1,0:T(8,128)S(1)} collective-permute-done((f32[512,128]{1,0:T(8,128)}, f32[512,128]{1,0:T(8,128)S(1)}, u32[]{:S(2)}, u32[]{:S(2)}) %collective-permute-start) | collective-permute-done | bytes 262176 | tf_op jit(solution)/shard_map/ppermute | solution.py:10
  84.7 8.1 %all-gather.5.cloned.1.call-done = f32[512,512]{1,0:T(8,128)} async-done(((f32[512,128]{1,0:T(8,128)}), f32[512,512]{1,0:T(8,128)}) %all-gather.5.cloned.1.call-update) | async-done | bytes 1048592 | tf_op jit(solution)/shard_map/all_gather | solution.py:44
  92.8 2.9 %convolution_select_fusion.2 = f32[512,128]{1,0:T(8,128)} fusion(f32[512,128]{1,0:T(8,128)} %copy-done, f32[512,512]{1,0:T(8,128)} %all-gather.5.cloned.1.call-done, f32[512,128]{1,0:T(8,128)S(1)} %collective-permute-done, pred[]{:T(512)S(6)} %ge.11), kind=kOutput, calls=%fused_computation.17 | convolution fusion | flops 402718720 | bytes 1835009 | tf_op jit(solution)/shard_map/dot_general | solution.py:14
  97.1 8.4 %collective-permute-done.1 = f32[512,128]{1,0:T(8,128)S(1)} collective-permute-done((f32[512,128]{1,0:T(8,128)}, f32[512,128]{1,0:T(8,128)S(1)}, u32[]{:S(2)}, u32[]{:S(2)}) %collective-permute-start.1) | collective-permute-done | bytes 262176 | tf_op jit(solution)/shard_map/ppermute | solution.py:10
  105.5 7.2 %all-gather.7.cloned.1.call-done = f32[512,512]{1,0:T(8,128)} async-done(((f32[512,128]{1,0:T(8,128)}), f32[512,512]{1,0:T(8,128)}) %all-gather.7.cloned.1.call-update) | async-done | bytes 1048592 | tf_op jit(solution)/shard_map/all_gather | solution.py:44
  112.7 2.9 %convolution_select_fusion.1 = f32[512,128]{1,0:T(8,128)} fusion(f32[512,128]{1,0:T(8,128)} %convolution_select_fusion.2, f32[512,512]{1,0:T(8,128)} %all-gather.7.cloned.1.call-done, f32[512,128]{1,0:T(8,128)S(1)} %collective-permute-done.1, pred[]{:T(512)S(6)} %ge.10), kind=kOutput, calls=%fused_computation.16 | convolution fusion | flops 402718720 | bytes 1835009 | tf_op jit(solution)/shard_map/dot_general | solution.py:14
  115.7 3.1 %collective-permute-start.3 = (f32[512]{0:T(512)S(1)}, f32[512]{0:T(512)S(1)}, u32[]{:S(2)}, u32[]{:S(2)}) collective-permute-start(f32[512]{0:T(512)S(1)} %get-tuple-element.108), channel_id=1, source_target_pairs={{0,4},{4,8},{8,12},{12,16},{16,20},{20,24},{24,28},{1,5},{5,9},{9,... | collective-permute-start | bytes 6152 | tf_op jit(solution)/shard_map/ppermute | solution.py:10
  120.9 2.2 %fusion.17 = f32[1,512]{1,0:T(1,128)S(1)} fusion(f32[512,512]{1,0:T(8,128)} %all-gather.5.cloned.1.call-done, f32[512,1]{0,1:T(1,128)S(1)} %bitcast.89), kind=kOutput, calls=%fused_computation.30 | convolution fusion | flops 3145728 | bytes 1052672 | tf_op jit(solution)/shard_map/dot_general | solution.py:14
  124.5 3.4 %collective-permute-done.4 = f32[512]{0:T(512)S(1)} collective-permute-done((f32[512]{0:T(512)S(1)}, f32[512]{0:T(512)S(1)}, u32[]{:S(2)}, u32[]{:S(2)}) %collective-permute-start.4) | collective-permute-done | bytes 2080 | tf_op jit(solution)/shard_map/ppermute | solution.py:10
  127.9 2.3 %fusion.18 = f32[1,512]{1,0:T(1,128)S(1)} fusion(f32[512,512]{1,0:T(8,128)} %all-gather.7.cloned.1.call-done, f32[512,1]{0,1:T(1,128)S(1)} %bitcast.90), kind=kOutput, calls=%fused_computation.31 | convolution fusion | flops 3145728 | bytes 1052672 | tf_op jit(solution)/shard_map/dot_general | solution.py:14
  137.6 11.9 %collective-permute-done.2 = f32[512,128]{1,0:T(8,128)S(1)} collective-permute-done((f32[512,128]{1,0:T(8,128)}, f32[512,128]{1,0:T(8,128)S(1)}, u32[]{:S(2)}, u32[]{:S(2)}) %collective-permute-start.2) | collective-permute-done | bytes 262176 | tf_op jit(solution)/shard_map/ppermute | solution.py:10
  149.5 2.2 %convolution_select_fusion = f32[512,128]{1,0:T(8,128)S(1)} fusion(f32[512,128]{1,0:T(8,128)} %convolution_select_fusion.1, f32[512,512]{1,0:T(8,128)} %all-gather.9.cloned.1.call-done, f32[512,128]{1,0:T(8,128)S(1)} %collective-permute-done.2, pred[]{:T(512)S(6)} %ge.9), kind=kOutput, calls=%fused_computation.15 | convolution fusion | flops 402718720 | bytes 1835009 | tf_op jit(solution)/shard_map/dot_general | solution.py:14
  152.1 5.5 %all-reduce = f32[512]{0:T(512)S(1)} all-reduce(f32[512]{0:T(512)S(1)} %bitcast.87), channel_id=2, replica_groups=mesh['tm'=8,'col'=4] {'col'}, use_global_device_ids=true, to_apply=%region_2.3.clone | all-reduce | flops 512 | bytes 4096
  159.8 3.1 %collective-permute-done.6 = f32[128]{0:T(128)S(1)} collective-permute-done((f32[128]{0:T(128)S(1)}, f32[128]{0:T(128)S(1)}, u32[]{:S(2)}, u32[]{:S(2)}) %collective-permute-start.6) | collective-permute-done | bytes 544 | tf_op jit(solution)/shard_map/ppermute | solution.py:10
  162.9 6.9 %all-gather = f32[4,1,128]{2,1,0:T(1,128)S(1)} all-gather(f32[1,1,128]{2,1,0:T(1,128)S(1)} %fusion.12), channel_id=1, replica_groups=mesh['tm'=8,'col'=4] {'col'}, dimensions={0}, use_global_device_ids=true | all-gather | bytes 2560 | tf_op jit(solution)/shard_map/all_gather | solution.py:56
  169.8 25.8 %while.27 = (s32[]{:T(128)}, f32[512]{0:T(512)S(1)}, f32[11,128]{1,0:T(8,128)S(1)}, f32[11,512,512]{2,1,0:T(8,128)}, f32[11,512]{1,0:T(8,128)S(1)}, /*index=5*/s32[]{:T(128)}, s32[]{:T(128)}, s32[]{:T(128)}) while((s32[]{:T(128)}, f32[512]{0:T(512)S(1)}, f32[11,128]{1,0:T(8,128)S(1)}, f32[11,512,512]{2,1,0:T(8,128)}, f32[11,512]{1,0:T(8,128)S(1)}, ...), condition=%wide.region_4.5_spmd, body=%wide.region_3.4_spmd.sunk | while | flops 3146242 | bytes 1065569 | solution.py:63
  172.1 2.2 %fusion.53 = f32[1,512]{1,0:T(1,128)S(1)} fusion(f32[512,1]{0,1:T(1,128)S(1)} %bitcast.83, f32[11,512,512]{2,1,0:T(8,128)} %get-tuple-element.241, s32[]{:T(128)} %get-tuple-element.230), kind=kOutput, calls=%fused_computation.9.clone.1 | convolution fusion | flops 3145728 | bytes 1053184 | tf_op jit(solution)/shard_map/while/body/eval_jaxpr/dot_general | solution.py:14
  174.5 2.2 %fusion.53 = f32[1,512]{1,0:T(1,128)S(1)} fusion(f32[512,1]{0,1:T(1,128)S(1)} %bitcast.83, f32[11,512,512]{2,1,0:T(8,128)} %get-tuple-element.241, s32[]{:T(128)} %get-tuple-element.230), kind=kOutput, calls=%fused_computation.9.clone.1 | convolution fusion | flops 3145728 | bytes 1053184 | tf_op jit(solution)/shard_map/while/body/eval_jaxpr/dot_general | solution.py:14
  176.8 2.2 %fusion.53 = f32[1,512]{1,0:T(1,128)S(1)} fusion(f32[512,1]{0,1:T(1,128)S(1)} %bitcast.83, f32[11,512,512]{2,1,0:T(8,128)} %get-tuple-element.241, s32[]{:T(128)} %get-tuple-element.230), kind=kOutput, calls=%fused_computation.9.clone.1 | convolution fusion | flops 3145728 | bytes 1053184 | tf_op jit(solution)/shard_map/while/body/eval_jaxpr/dot_general | solution.py:14
  179.2 2.2 %fusion.53 = f32[1,512]{1,0:T(1,128)S(1)} fusion(f32[512,1]{0,1:T(1,128)S(1)} %bitcast.83, f32[11,512,512]{2,1,0:T(8,128)} %get-tuple-element.241, s32[]{:T(128)} %get-tuple-element.230), kind=kOutput, calls=%fused_computation.9.clone.1 | convolution fusion | flops 3145728 | bytes 1053184 | tf_op jit(solution)/shard_map/while/body/eval_jaxpr/dot_general | solution.py:14
  181.5 2.2 %fusion.53 = f32[1,512]{1,0:T(1,128)S(1)} fusion(f32[512,1]{0,1:T(1,128)S(1)} %bitcast.83, f32[11,512,512]{2,1,0:T(8,128)} %get-tuple-element.241, s32[]{:T(128)} %get-tuple-element.230), kind=kOutput, calls=%fused_computation.9.clone.1 | convolution fusion | flops 3145728 | bytes 1053184 | tf_op jit(solution)/shard_map/while/body/eval_jaxpr/dot_general | solution.py:14
  183.9 2.2 %fusion.53 = f32[1,512]{1,0:T(1,128)S(1)} fusion(f32[512,1]{0,1:T(1,128)S(1)} %bitcast.83, f32[11,512,512]{2,1,0:T(8,128)} %get-tuple-element.241, s32[]{:T(128)} %get-tuple-element.230), kind=kOutput, calls=%fused_computation.9.clone.1 | convolution fusion | flops 3145728 | bytes 1053184 | tf_op jit(solution)/shard_map/while/body/eval_jaxpr/dot_general | solution.py:14
  186.2 2.2 %fusion.53 = f32[1,512]{1,0:T(1,128)S(1)} fusion(f32[512,1]{0,1:T(1,128)S(1)} %bitcast.83, f32[11,512,512]{2,1,0:T(8,128)} %get-tuple-element.241, s32[]{:T(128)} %get-tuple-element.230), kind=kOutput, calls=%fused_computation.9.clone.1 | convolution fusion | flops 3145728 | bytes 1053184 | tf_op jit(solution)/shard_map/while/body/eval_jaxpr/dot_general | solution.py:14
  188.6 2.2 %fusion.53 = f32[1,512]{1,0:T(1,128)S(1)} fusion(f32[512,1]{0,1:T(1,128)S(1)} %bitcast.83, f32[11,512,512]{2,1,0:T(8,128)} %get-tuple-element.241, s32[]{:T(128)} %get-tuple-element.230), kind=kOutput, calls=%fused_computation.9.clone.1 | convolution fusion | flops 3145728 | bytes 1053184 | tf_op jit(solution)/shard_map/while/body/eval_jaxpr/dot_general | solution.py:14
  190.9 2.2 %fusion.53 = f32[1,512]{1,0:T(1,128)S(1)} fusion(f32[512,1]{0,1:T(1,128)S(1)} %bitcast.83, f32[11,512,512]{2,1,0:T(8,128)} %get-tuple-element.241, s32[]{:T(128)} %get-tuple-element.230), kind=kOutput, calls=%fused_computation.9.clone.1 | convolution fusion | flops 3145728 | bytes 1053184 | tf_op jit(solution)/shard_map/while/body/eval_jaxpr/dot_general | solution.py:14
  193.3 2.2 %fusion.53 = f32[1,512]{1,0:T(1,128)S(1)} fusion(f32[512,1]{0,1:T(1,128)S(1)} %bitcast.83, f32[11,512,512]{2,1,0:T(8,128)} %get-tuple-element.241, s32[]{:T(128)} %get-tuple-element.230), kind=kOutput, calls=%fused_computation.9.clone.1 | convolution fusion | flops 3145728 | bytes 1053184 | tf_op jit(solution)/shard_map/while/body/eval_jaxpr/dot_general | solution.py:14
  (119 shorter events, 26.2 us)
Async XLA Ops:
  6.5 86.3 %all-gather.5.cloned.1.call-start = ((), (), s32[]{:S(2)}) async-start(), calls=%async_computation | async-start | bytes 1310720 | tf_op jit(solution)/shard_map/all_gather | solution.py:44
  6.5 17.6 %copy-start.1 = (f32[12,512]{1,0:T(8,128)S(1)}, f32[12,512]{1,0:T(8,128)}, u32[]{:S(2)}) copy-start(f32[12,512]{1,0:T(8,128)} %param.8) | copy-start | bytes 73732
  6.5 17.6 %slice-start = ((f32[12,512,512]{2,1,0:T(8,128)}), f32[1,512,512]{2,1,0:T(8,128)S(1)}, s32[]{:S(2)}) async-start(f32[12,512,512]{2,1,0:T(8,128)} %param.7), calls=%async_computation.3 | async-start | bytes 2097152 | tf_op jit(solution)/shard_map/slice | solution.py:32
  6.5 17.7 %slice-start.1 = ((f32[12,512]{1,0:T(8,128)}), f32[1,512]{1,0:T(1,128)S(1)}, s32[]{:S(2)}) async-start(f32[12,512]{1,0:T(8,128)} %param.8), calls=%async_computation.4 | async-start | bytes 4096 | tf_op jit(solution)/shard_map/slice | solution.py:32
  24.1 107.3 %copy-start.3 = (u32[32]{0:T(128)S(1)}, u32[32]{0:T(128)}, u32[]{:S(2)}) copy-start(u32[32]{0:T(128)} %constant.58) | copy-start | bytes 388
  24.2 127.5 %copy-start.2 = (f32[128]{0:T(128)S(1)}, f32[128]{0:T(128)}, u32[]{:S(2)}) copy-start(f32[128]{0:T(128)} %param.9) | copy-start | bytes 1540
  73.7 0.7 copy-start
  74.5 38.3 %all-gather.7.cloned.1.call-start = ((), (), s32[]{:S(2)}) async-start(), calls=%async_computation.1 | async-start | bytes 1310720 | tf_op jit(solution)/shard_map/all_gather | solution.py:44
  74.5 10.2 %collective-permute-start = (f32[512,128]{1,0:T(8,128)}, f32[512,128]{1,0:T(8,128)S(1)}, u32[]{:S(2)}, u32[]{:S(2)}) collective-permute-start(f32[512,128]{1,0:T(8,128)} %copy-done), channel_id=1, source_target_pairs={{0,4},{4,8},{8,12},{12,16},{16,20},{20,24},{24,28},{1,5},{5,9},{9,... | collective-permute-start | bytes 786440 | tf_op jit(solution)/shard_map/ppermute | solution.py:10
  95.8 39.6 %all-gather.9.cloned.1.call-start = ((), (), s32[]{:S(2)}) async-start(), calls=%async_computation.2 | async-start | bytes 1310720 | tf_op jit(solution)/shard_map/all_gather | solution.py:44
  95.8 9.7 %collective-permute-start.1 = (f32[512,128]{1,0:T(8,128)}, f32[512,128]{1,0:T(8,128)S(1)}, u32[]{:S(2)}, u32[]{:S(2)}) collective-permute-start(f32[512,128]{1,0:T(8,128)} %convolution_select_fusion.2), channel_id=1, source_target_pairs={{0,8},{4,12},{8,16},{12,20},{16,24},{20,28},{1,9},{5,13},{9,17},{1... | collective-permute-start | bytes 786440 | tf_op jit(solution)/shard_map/ppermute | solution.py:10
  115.7 5.2 %collective-permute-start.3 = (f32[512]{0:T(512)S(1)}, f32[512]{0:T(512)S(1)}, u32[]{:S(2)}, u32[]{:S(2)}) collective-permute-start(f32[512]{0:T(512)S(1)} %get-tuple-element.108), channel_id=1, source_target_pairs={{0,4},{4,8},{8,12},{12,16},{16,20},{20,24},{24,28},{1,5},{5,9},{9,... | collective-permute-start | bytes 6152 | tf_op jit(solution)/shard_map/ppermute | solution.py:10
  123.2 4.7 %collective-permute-start.4 = (f32[512]{0:T(512)S(1)}, f32[512]{0:T(512)S(1)}, u32[]{:S(2)}, u32[]{:S(2)}) collective-permute-start(f32[512]{0:T(512)S(1)} %add_select_fusion.2), channel_id=1, source_target_pairs={{0,8},{4,12},{8,16},{12,20},{16,24},{20,28},{1,9},{5,13},{9,17},{1... | collective-permute-start | bytes 6152 | tf_op jit(solution)/shard_map/ppermute | solution.py:10
  130.2 5.2 %collective-permute-start.5 = (f32[512]{0:T(512)S(1)}, f32[512]{0:T(512)S(1)}, u32[]{:S(2)}, u32[]{:S(2)}) collective-permute-start(f32[512]{0:T(512)S(1)} %add_select_fusion.1), channel_id=1, source_target_pairs={{0,16},{4,20},{8,24},{12,28},{1,17},{5,21},{9,25},{13,29},{2,18},{... | collective-permute-start | bytes 6152 | tf_op jit(solution)/shard_map/ppermute | solution.py:10
  132.7 16.8 %collective-permute-start.2 = (f32[512,128]{1,0:T(8,128)}, f32[512,128]{1,0:T(8,128)S(1)}, u32[]{:S(2)}, u32[]{:S(2)}) collective-permute-start(f32[512,128]{1,0:T(8,128)} %convolution_select_fusion.1), channel_id=1, source_target_pairs={{0,16},{4,20},{8,24},{12,28},{1,17},{5,21},{9,25},{13,29},{2,18},{... | collective-permute-start | bytes 786440 | tf_op jit(solution)/shard_map/ppermute | solution.py:10
  157.7 5.2 %collective-permute-start.6 = (f32[128]{0:T(128)S(1)}, f32[128]{0:T(128)S(1)}, u32[]{:S(2)}, u32[]{:S(2)}) collective-permute-start(f32[128]{0:T(128)S(1)} %dynamic-slice_add_fusion), channel_id=1, source_target_pairs={{0,4},{4,8},{8,12},{12,16},{16,20},{20,24},{24,28},{1,5},{5,9},{9,... | collective-permute-start | bytes 1544 | tf_op jit(solution)/shard_map/ppermute | solution.py:10
Sparse Core Ops, SparseCore 0:
  74.6 18.1 all-gather.4
  95.9 16.8 all-gather.6
  115.8 16.8 all-gather.8
where the time goes:
time: 205 us; the launch traced here: 203 us
  matrix products  87.8 us (43%)
  waiting for transfers between devices  52.8 us (26%)
  local copies, waits for them, and re-layouts  20.7 us (10%)
  between operations  14 us (7%)
  starting transfers between devices  13.6 us (7%)
  blocking collectives  12.4 us (6%)
    dot_general x40, matrix products, matmul(): jnp.dot(left, right, precision=lax.Precision.HIGHEST, preferred_element_t...  87.8 us
    ppermute x7, waiting for transfers between devices, from_behind(): return lax.ppermute(block, axis, route)  37.4 us
    slice x1, local copies, waits for them, and re-layouts, body(): jacobians[:-1]  17.6 us
    all_gather x3, waiting for transfers between devices, body(): lax.all_gather(acc_map, 'col', axis=1, tiled=True)  15.3 us
    ppermute x7, starting transfers between devices, from_behind(): return lax.ppermute(block, axis, route)  13.5 us
    all_gather x1, blocking collectives, body(): start_full = lax.all_gather(start_mine, 'col', axis=0, tiled=True)  6.9 us
    unnamed x1, blocking collectives  5.5 us
  transfers between devices with their start and end apart: 10, of which 9 were waited for; matrix products, arithmetic and copies ran while one was open for 4% of the time, Pallas kernels for 0%

commit v1 on v0

--- a/solution.py
+++ b/solution.py
@@ -1,7 +1,23 @@
+import functools
 import jax
 import jax.numpy as jnp
 from jax import lax
 from jax.sharding import PartitionSpec as P
+from jax.lax import all_to_all, axis_size
+
+
+def step_on_outputs(xin, net_axis, row_dim):
+    degree = axis_size(net_axis)
+    return all_to_all(
+        jnp.tile(xin, [degree if s == row_dim else 1 for s in range(xin.ndim)]),
+        axis_name=net_axis,
+        split_axis=row_dim,
+        concat_axis=row_dim,
+        tiled=True,
+    )
+
+
+map_results = functools.partial(step_on_outputs, net_axis="col", row_dim=1)
 
 
 def from_behind(block, axis, distance):
@@ -40,9 +56,7 @@
             return (matmul(col_block, recv_map), running[1] + matmul(col_block, recv_off))
 
         new_map, new_off = fold_columns(
-            (jnp.zeros_like(acc_map), acc_off),
-            lax.all_gather(acc_map, "col", axis=1, tiled=True),
-            jnp.int32(0),
+            (jnp.zeros_like(acc_map), acc_off), map_results(acc_map), jnp.int32(0)
         )
         active = segment_index >= distance
         acc_map = jnp.where(active, new_map, acc_map)

time: 205 us -> 190 us (0.927)
  starting transfers between devices: 13.6 us -> 27.7 us
  waiting for transfers between devices: 52.8 us -> 39 us
  between operations: 14 us -> 0.91 us
  matrix products: 87.8 us -> 81.4 us
  local copies, waits for them, and re-layouts: 20.7 us -> 24.2 us
    all_to_all x0 -> x3, waiting for transfers between devices: none -> 23.1 us  [step_on_outputs(): all_to_all(jnp.tile(xin, [degree if s == row_dim else 1 for s in range(xi...]
    ppermute x7, waiting for transfers between devices: 37.4 us -> 15.9 us  [from_behind(): return lax.ppermute(block, axis, route)]
    all_gather x3 -> x0, waiting for transfers between devices: 15.3 us -> none  [body(): lax.all_gather(acc_map, 'col', axis=1, tiled=True)]
    all_to_all x0 -> x3, starting transfers between devices: none -> 13.2 us  [step_on_outputs(): all_to_all(jnp.tile(xin, [degree if s == row_dim else 1 for s in range(xi...]
    dot_general x40, matrix products: 87.8 us -> 81.4 us  [matmul(): jnp.dot(left, right, precision=lax.Precision.HIGHEST, preferred_element_t...]
    another operation x0 -> x3, local copies, waits for them, and re-layouts: none -> 3.22 us  [step_on_outputs(): jnp.tile(xin, [degree if s == row_dim else 1 for s in range(xin.ndim)])]
  transfers between devices with their start and end apart: 10 -> 10, of which waited for: 9 -> 6; matrix products, arithmetic and copies ran while one was open for 4% -> 4% of each run, Pallas kernels for 0% -> 0%
where the time goes in v1:
time: 190 us; the launch traced here: 188 us
  matrix products  81.4 us (43%)
  waiting for transfers between devices  39 us (21%)
  starting transfers between devices  27.7 us (15%)
  local copies, waits for them, and re-layouts  24.2 us (13%)
  blocking collectives  13.5 us (7%)
    dot_general x40, matrix products, matmul(): jnp.dot(left, right, precision=lax.Precision.HIGHEST, preferred_element_t...  81.4 us
    all_to_all x3, waiting for transfers between devices, step_on_outputs(): all_to_all(jnp.tile(xin, [degree if s == row_dim else 1 for s in range(xi...  23.1 us
    slice x1, local copies, waits for them, and re-layouts, body(): jacobians[:-1]  17.5 us
    ppermute x7, waiting for transfers between devices, from_behind(): return lax.ppermute(block, axis, route)  15.9 us
    ppermute x7, starting transfers between devices, from_behind(): return lax.ppermute(block, axis, route)  14.5 us
    all_to_all x3, starting transfers between devices, step_on_outputs(): all_to_all(jnp.tile(xin, [degree if s == row_dim else 1 for s in range(xi...  13.2 us
    all_gather x1, blocking collectives, body(): start_full = lax.all_gather(start_mine, 'col', axis=0, tiled=True)  8.01 us
    unnamed x1, blocking collectives  5.51 us
  transfers between devices with their start and end apart: 10, of which 6 were waited for; matrix products, arithmetic and copies ran while one was open for 4% of the time, Pallas kernels for 0%

profile of v1, /device:TPU:25, one launch (start us, length us, event | category | flops | bytes accessed | tf_op | source)
XLA Modules:
  0.0 188.2 jit_solution(3735531292592620661)
XLA Ops:
  0.0 17.5 %fusion.15 = (f32[11,512,512]{2,1,0:T(8,128)}, f32[11,512,512]{2,1,0:T(8,128)}) fusion(f32[12,512,512]{2,1,0:T(8,128)} %param.7), kind=kLoop, calls=%fused_computation.28 | loop fusion | bytes 46137344 | tf_op jit(solution)/shard_map/slice | solution.py:77
  17.6 49.5 %while.26 = (s32[]{:T(128)}, f32[512,128]{1,0:T(8,128)S(1)}, f32[512]{0:T(512)S(1)}, f32[11,512,512]{2,1,0:T(8,128)}, f32[11,512]{1,0:T(8,128)S(1)}, /*index=5*/s32[]{:T(128)}) while((s32[]{:T(128)}, f32[512,128]{1,0:T(8,128)S(1)}, f32[512]{0:T(512)S(1)}, f32[11,512,512]{2,1,0:T(8,128)}, f32[11,512]{1,0:T(8,128)S(1)}, ...), condition=%wide.region_1.2_spmd, body=%wide.region_0.1_spmd.sunk | while | flops 405799424 | bytes 3161161 | solution.py:47
  17.6 2.2 %fusion.50 = f32[1,512]{1,0:T(1,128)S(1)} fusion(f32[512,1]{0,1:T(1,128)S(1)} %bitcast.89, f32[11,512,512]{2,1,0:T(8,128)} %get-tuple-element.219, s32[]{:T(128)} %get-tuple-element.210), kind=kOutput, calls=%fused_computation.clone.1 | convolution fusion | flops 3145728 | bytes 1053184 | tf_op jit(solution)/shard_map/while/body/eval_jaxpr/dot_general | solution.py:30
  19.9 2.2 %fusion.49 = f32[512,128]{1,0:T(8,128)S(1)} fusion(f32[512,128]{1,0:T(8,128)S(1)} %copy.27, f32[11,512,512]{2,1,0:T(8,128)} %get-tuple-element.219, s32[]{:T(128)} %get-tuple-element.210), kind=kOutput, calls=%fused_computation.2.clone.1 | convolution fusion | flops 402653184 | bytes 1573376 | tf_op jit(solution)/shard_map/while/body/eval_jaxpr/dot_general | solution.py:30
  22.1 2.2 %fusion.50 = f32[1,512]{1,0:T(1,128)S(1)} fusion(f32[512,1]{0,1:T(1,128)S(1)} %bitcast.89, f32[11,512,512]{2,1,0:T(8,128)} %get-tuple-element.219, s32[]{:T(128)} %get-tuple-element.210), kind=kOutput, calls=%fused_computation.clone.1 | convolution fusion | flops 3145728 | bytes 1053184 | tf_op jit(solution)/shard_map/while/body/eval_jaxpr/dot_general | solution.py:30
  24.4 2.2 %fusion.49 = f32[512,128]{1,0:T(8,128)S(1)} fusion(f32[512,128]{1,0:T(8,128)S(1)} %copy.27, f32[11,512,512]{2,1,0:T(8,128)} %get-tuple-element.219, s32[]{:T(128)} %get-tuple-element.210), kind=kOutput, calls=%fused_computation.2.clone.1 | convolution fusion | flops 402653184 | bytes 1573376 | tf_op jit(solution)/shard_map/while/body/eval_jaxpr/dot_general | solution.py:30
  26.6 2.2 %fusion.50 = f32[1,512]{1,0:T(1,128)S(1)} fusion(f32[512,1]{0,1:T(1,128)S(1)} %bitcast.89, f32[11,512,512]{2,1,0:T(8,128)} %get-tuple-element.219, s32[]{:T(128)} %get-tuple-element.210), kind=kOutput, calls=%fused_computation.clone.1 | convolution fusion | flops 3145728 | bytes 1053184 | tf_op jit(solution)/shard_map/while/body/eval_jaxpr/dot_general | solution.py:30
  28.9 2.2 %fusion.49 = f32[512,128]{1,0:T(8,128)S(1)} fusion(f32[512,128]{1,0:T(8,128)S(1)} %copy.27, f32[11,512,512]{2,1,0:T(8,128)} %get-tuple-element.219, s32[]{:T(128)} %get-tuple-element.210), kind=kOutput, calls=%fused_computation.2.clone.1 | convolution fusion | flops 402653184 | bytes 1573376 | tf_op jit(solution)/shard_map/while/body/eval_jaxpr/dot_general | solution.py:30
  31.1 2.2 %fusion.50 = f32[1,512]{1,0:T(1,128)S(1)} fusion(f32[512,1]{0,1:T(1,128)S(1)} %bitcast.89, f32[11,512,512]{2,1,0:T(8,128)} %get-tuple-element.219, s32[]{:T(128)} %get-tuple-element.210), kind=kOutput, calls=%fused_computation.clone.1 | convolution fusion | flops 3145728 | bytes 1053184 | tf_op jit(solution)/shard_map/while/body/eval_jaxpr/dot_general | solution.py:30
  33.4 2.2 %fusion.49 = f32[512,128]{1,0:T(8,128)S(1)} fusion(f32[512,128]{1,0:T(8,128)S(1)} %copy.27, f32[11,512,512]{2,1,0:T(8,128)} %get-tuple-element.219, s32[]{:T(128)} %get-tuple-element.210), kind=kOutput, calls=%fused_computation.2.clone.1 | convolution fusion | flops 402653184 | bytes 1573376 | tf_op jit(solution)/shard_map/while/body/eval_jaxpr/dot_general | solution.py:30
  35.6 2.2 %fusion.50 = f32[1,512]{1,0:T(1,128)S(1)} fusion(f32[512,1]{0,1:T(1,128)S(1)} %bitcast.89, f32[11,512,512]{2,1,0:T(8,128)} %get-tuple-element.219, s32[]{:T(128)} %get-tuple-element.210), kind=kOutput, calls=%fused_computation.clone.1 | convolution fusion | flops 3145728 | bytes 1053184 | tf_op jit(solution)/shard_map/while/body/eval_jaxpr/dot_general | solution.py:30
  37.9 2.2 %fusion.49 = f32[512,128]{1,0:T(8,128)S(1)} fusion(f32[512,128]{1,0:T(8,128)S(1)} %copy.27, f32[11,512,512]{2,1,0:T(8,128)} %get-tuple-element.219, s32[]{:T(128)} %get-tuple-element.210), kind=kOutput, calls=%fused_computation.2.clone.1 | convolution fusion | flops 402653184 | bytes 1573376 | tf_op jit(solution)/shard_map/while/body/eval_jaxpr/dot_general | solution.py:30
  40.1 2.2 %fusion.50 = f32[1,512]{1,0:T(1,128)S(1)} fusion(f32[512,1]{0,1:T(1,128)S(1)} %bitcast.89, f32[11,512,512]{2,1,0:T(8,128)} %get-tuple-element.219, s32[]{:T(128)} %get-tuple-element.210), kind=kOutput, calls=%fused_computation.clone.1 | convolution fusion | flops 3145728 | bytes 1053184 | tf_op jit(solution)/shard_map/while/body/eval_jaxpr/dot_general | solution.py:30
  42.4 2.2 %fusion.49 = f32[512,128]{1,0:T(8,128)S(1)} fusion(f32[512,128]{1,0:T(8,128)S(1)} %copy.27, f32[11,512,512]{2,1,0:T(8,128)} %get-tuple-element.219, s32[]{:T(128)} %get-tuple-element.210), kind=kOutput, calls=%fused_computation.2.clone.1 | convolution fusion | flops 402653184 | bytes 1573376 | tf_op jit(solution)/shard_map/while/body/eval_jaxpr/dot_general | solution.py:30
  44.6 2.2 %fusion.50 = f32[1,512]{1,0:T(1,128)S(1)} fusion(f32[512,1]{0,1:T(1,128)S(1)} %bitcast.89, f32[11,512,512]{2,1,0:T(8,128)} %get-tuple-element.219, s32[]{:T(128)} %get-tuple-element.210), kind=kOutput, calls=%fused_computation.clone.1 | convolution fusion | flops 3145728 | bytes 1053184 | tf_op jit(solution)/shard_map/while/body/eval_jaxpr/dot_general | solution.py:30
  46.9 2.2 %fusion.49 = f32[512,128]{1,0:T(8,128)S(1)} fusion(f32[512,128]{1,0:T(8,128)S(1)} %copy.27, f32[11,512,512]{2,1,0:T(8,128)} %get-tuple-element.219, s32[]{:T(128)} %get-tuple-element.210), kind=kOutput, calls=%fused_computation.2.clone.1 | convolution fusion | flops 402653184 | bytes 1573376 | tf_op jit(solution)/shard_map/while/body/eval_jaxpr/dot_general | solution.py:30
  49.1 2.2 %fusion.50 = f32[1,512]{1,0:T(1,128)S(1)} fusion(f32[512,1]{0,1:T(1,128)S(1)} %bitcast.89, f32[11,512,512]{2,1,0:T(8,128)} %get-tuple-element.219, s32[]{:T(128)} %get-tuple-element.210), kind=kOutput, calls=%fused_computation.clone.1 | convolution fusion | flops 3145728 | bytes 1053184 | tf_op jit(solution)/shard_map/while/body/eval_jaxpr/dot_general | solution.py:30
  51.4 2.2 %fusion.49 = f32[512,128]{1,0:T(8,128)S(1)} fusion(f32[512,128]{1,0:T(8,128)S(1)} %copy.27, f32[11,512,512]{2,1,0:T(8,128)} %get-tuple-element.219, s32[]{:T(128)} %get-tuple-element.210), kind=kOutput, calls=%fused_computation.2.clone.1 | convolution fusion | flops 402653184 | bytes 1573376 | tf_op jit(solution)/shard_map/while/body/eval_jaxpr/dot_general | solution.py:30
  55.9 2.2 %fusion.49 = f32[512,128]{1,0:T(8,128)S(1)} fusion(f32[512,128]{1,0:T(8,128)S(1)} %copy.27, f32[11,512,512]{2,1,0:T(8,128)} %get-tuple-element.219, s32[]{:T(128)} %get-tuple-element.210), kind=kOutput, calls=%fused_computation.2.clone.1 | convolution fusion | flops 402653184 | bytes 1573376 | tf_op jit(solution)/shard_map/while/body/eval_jaxpr/dot_general | solution.py:30
  58.1 2.2 %fusion.50 = f32[1,512]{1,0:T(1,128)S(1)} fusion(f32[512,1]{0,1:T(1,128)S(1)} %bitcast.89, f32[11,512,512]{2,1,0:T(8,128)} %get-tuple-element.219, s32[]{:T(128)} %get-tuple-element.210), kind=kOutput, calls=%fused_computation.clone.1 | convolution fusion | flops 3145728 | bytes 1053184 | tf_op jit(solution)/shard_map/while/body/eval_jaxpr/dot_general | solution.py:30
  60.4 2.2 %fusion.49 = f32[512,128]{1,0:T(8,128)S(1)} fusion(f32[512,128]{1,0:T(8,128)S(1)} %copy.27, f32[11,512,512]{2,1,0:T(8,128)} %get-tuple-element.219, s32[]{:T(128)} %get-tuple-element.210), kind=kOutput, calls=%fused_computation.2.clone.1 | convolution fusion | flops 402653184 | bytes 1573376 | tf_op jit(solution)/shard_map/while/body/eval_jaxpr/dot_general | solution.py:30
  62.6 2.2 %fusion.50 = f32[1,512]{1,0:T(1,128)S(1)} fusion(f32[512,1]{0,1:T(1,128)S(1)} %bitcast.89, f32[11,512,512]{2,1,0:T(8,128)} %get-tuple-element.219, s32[]{:T(128)} %get-tuple-element.210), kind=kOutput, calls=%fused_computation.clone.1 | convolution fusion | flops 3145728 | bytes 1053184 | tf_op jit(solution)/shard_map/while/body/eval_jaxpr/dot_general | solution.py:30
  64.9 2.2 %fusion.49 = f32[512,128]{1,0:T(8,128)S(1)} fusion(f32[512,128]{1,0:T(8,128)S(1)} %copy.27, f32[11,512,512]{2,1,0:T(8,128)} %get-tuple-element.219, s32[]{:T(128)} %get-tuple-element.210), kind=kOutput, calls=%fused_computation.2.clone.1 | convolution fusion | flops 402653184 | bytes 1573376 | tf_op jit(solution)/shard_map/while/body/eval_jaxpr/dot_general | solution.py:30
  68.2 4.3 %all-to-all-start = ((f32[512,4,128]{2,0,1:T(8,128)}), f32[512,4,128]{2,0,1:T(8,128)S(1)}, u32[]{:S(2)}, u32[]{:S(2)}) async-start(f32[512,4,128]{2,0,1:T(8,128)} %tile.6), calls=%async_computation | async-start | bytes 2097152 | tf_op jit(solution)/shard_map/all_to_all | solution.py:11
  72.5 3.1 %collective-permute-start = (f32[512,128]{1,0:T(8,128)S(1)}, f32[512,128]{1,0:T(8,128)S(1)}, u32[]{:S(2)}, u32[]{:S(2)}) collective-permute-start(f32[512,128]{1,0:T(8,128)S(1)} %get-tuple-element.107), channel_id=1, source_target_pairs={{0,4},{4,8},{8,12},{12,16},{16,20},{20,24},{24,28},{1,5},{5,9},{9,... | collective-permute-start | bytes 786440 | tf_op jit(solution)/shard_map/ppermute | solution.py:26
  75.6 10.3 %all-to-all-done = f32[512,4,128]{2,0,1:T(8,128)S(1)} async-done(((f32[512,4,128]{2,0,1:T(8,128)}), f32[512,4,128]{2,0,1:T(8,128)S(1)}, u32[]{:S(2)}, u32[]{:S(2)}) %all-to-all-start) | async-done | bytes 1048608 | tf_op jit(solution)/shard_map/all_to_all | solution.py:11
  89.2 4.5 %all-to-all-start.1 = ((f32[512,4,128]{2,0,1:T(8,128)}), f32[512,4,128]{2,0,1:T(8,128)S(1)}, u32[]{:S(2)}, u32[]{:S(2)}) async-start(f32[512,4,128]{2,0,1:T(8,128)} %tile.7), calls=%async_computation.1 | async-start | bytes 2097152 | tf_op jit(solution)/shard_map/all_to_all | solution.py:11
  95.0 3.1 %collective-permute-start.3 = (f32[512]{0:T(512)S(1)}, f32[512]{0:T(512)S(1)}, u32[]{:S(2)}, u32[]{:S(2)}) collective-permute-start(f32[512]{0:T(512)S(1)} %get-tuple-element.108), channel_id=1, source_target_pairs={{0,4},{4,8},{8,12},{12,16},{16,20},{20,24},{24,28},{1,5},{5,9},{9,... | collective-permute-start | bytes 6152 | tf_op jit(solution)/shard_map/ppermute | solution.py:26
  98.1 9.0 %all-to-all-done.1 = f32[512,4,128]{2,0,1:T(8,128)S(1)} async-done(((f32[512,4,128]{2,0,1:T(8,128)}), f32[512,4,128]{2,0,1:T(8,128)S(1)}, u32[]{:S(2)}, u32[]{:S(2)}) %all-to-all-start.1) | async-done | bytes 1048608 | tf_op jit(solution)/shard_map/all_to_all | solution.py:11
  107.5 2.8 %convolution_select_fusion.1 = f32[512,128]{1,0:T(8,128)S(1)} fusion(f32[512,128]{1,0:T(8,128)} %copy-done, f32[512,512]{0,1:T(8,128)S(1)} %bitcast.81, f32[512,128]{1,0:T(8,128)} %collective-permute-done.1, pred[]{:T(512)S(6)} %ge.10), kind=kOutput, calls=%fused_computation.16 | convolution fusion | flops 402718720 | bytes 1835009 | tf_op jit(solution)/shard_map/dot_general | solution.py:30
  111.4 4.5 %all-to-all-start.2 = ((f32[512,4,128]{2,0,1:T(8,128)}), f32[512,4,128]{2,0,1:T(8,128)S(1)}, u32[]{:S(2)}, u32[]{:S(2)}) async-start(f32[512,4,128]{2,0,1:T(8,128)} %tile.8), calls=%async_computation.2 | async-start | bytes 2097152 | tf_op jit(solution)/shard_map/all_to_all | solution.py:11
  117.8 3.3 %collective-permute-done.4 = f32[512]{0:T(512)S(1)} collective-permute-done((f32[512]{0:T(512)S(1)}, f32[512]{0:T(512)S(1)}, u32[]{:S(2)}, u32[]{:S(2)}) %collective-permute-start.4) | collective-permute-done | bytes 2080 | tf_op jit(solution)/shard_map/ppermute | solution.py:26
  125.6 3.7 %all-to-all-done.2 = f32[512,4,128]{2,0,1:T(8,128)S(1)} async-done(((f32[512,4,128]{2,0,1:T(8,128)}), f32[512,4,128]{2,0,1:T(8,128)S(1)}, u32[]{:S(2)}, u32[]{:S(2)}) %all-to-all-start.2) | async-done | bytes 1048608 | tf_op jit(solution)/shard_map/all_to_all | solution.py:11
  130.3 10.5 %collective-permute-done.2 = f32[512,128]{1,0:T(8,128)S(1)} collective-permute-done((f32[512,128]{1,0:T(8,128)S(1)}, f32[512,128]{1,0:T(8,128)S(1)}, u32[]{:S(2)}, u32[]{:S(2)}) %collective-permute-start.2) | collective-permute-done | bytes 262176 | tf_op jit(solution)/shard_map/ppermute | solution.py:26
  143.0 5.5 %all-reduce = f32[512]{0:T(512)S(1)} all-reduce(f32[512]{0:T(512)S(1)} %bitcast.96), channel_id=2, replica_groups=mesh['tm'=8,'col'=4] {'col'}, use_global_device_ids=true, to_apply=%region_2.3.clone | all-reduce | flops 512 | bytes 4096
  148.6 3.1 %collective-permute-start.6 = (f32[128]{0:T(128)S(1)}, f32[128]{0:T(128)S(1)}, u32[]{:S(2)}, u32[]{:S(2)}) collective-permute-start(f32[128]{0:T(128)S(1)} %dynamic-slice_add_fusion), channel_id=1, source_target_pairs={{0,4},{4,8},{8,12},{12,16},{16,20},{20,24},{24,28},{1,5},{5,9},{9,... | collective-permute-start | bytes 1544 | tf_op jit(solution)/shard_map/ppermute | solution.py:26
  153.8 8.0 %all-gather = f32[4,1,128]{2,1,0:T(1,128)S(1)} all-gather(f32[1,1,128]{2,1,0:T(1,128)S(1)} %fusion.12), channel_id=1, replica_groups=mesh['tm'=8,'col'=4] {'col'}, dimensions={0}, use_global_device_ids=true | all-gather | bytes 2560 | tf_op jit(solution)/shard_map/all_gather | solution.py:70
  161.8 25.8 %while.27 = (s32[]{:T(128)}, f32[512]{0:T(512)S(1)}, f32[11,128]{1,0:T(8,128)S(1)}, f32[11,512,512]{2,1,0:T(8,128)}, f32[11,512]{1,0:T(8,128)S(1)}, /*index=5*/s32[]{:T(128)}, s32[]{:T(128)}, s32[]{:T(128)}) while((s32[]{:T(128)}, f32[512]{0:T(512)S(1)}, f32[11,128]{1,0:T(8,128)S(1)}, f32[11,512,512]{2,1,0:T(8,128)}, f32[11,512]{1,0:T(8,128)S(1)}, ...), condition=%wide.region_4.5_spmd, body=%wide.region_3.4_spmd.sunk | while | flops 3146242 | bytes 1065569 | solution.py:77
  164.1 2.2 %fusion.53 = f32[1,512]{1,0:T(1,128)S(1)} fusion(f32[512,1]{0,1:T(1,128)S(1)} %bitcast.92, f32[11,512,512]{2,1,0:T(8,128)} %get-tuple-element.241, s32[]{:T(128)} %get-tuple-element.230), kind=kOutput, calls=%fused_computation.9.clone.1 | convolution fusion | flops 3145728 | bytes 1053184 | tf_op jit(solution)/shard_map/while/body/eval_jaxpr/dot_general | solution.py:30
  166.5 2.2 %fusion.53 = f32[1,512]{1,0:T(1,128)S(1)} fusion(f32[512,1]{0,1:T(1,128)S(1)} %bitcast.92, f32[11,512,512]{2,1,0:T(8,128)} %get-tuple-element.241, s32[]{:T(128)} %get-tuple-element.230), kind=kOutput, calls=%fused_computation.9.clone.1 | convolution fusion | flops 3145728 | bytes 1053184 | tf_op jit(solution)/shard_map/while/body/eval_jaxpr/dot_general | solution.py:30
  168.8 2.2 %fusion.53 = f32[1,512]{1,0:T(1,128)S(1)} fusion(f32[512,1]{0,1:T(1,128)S(1)} %bitcast.92, f32[11,512,512]{2,1,0:T(8,128)} %get-tuple-element.241, s32[]{:T(128)} %get-tuple-element.230), kind=kOutput, calls=%fused_computation.9.clone.1 | convolution fusion | flops 3145728 | bytes 1053184 | tf_op jit(solution)/shard_map/while/body/eval_jaxpr/dot_general | solution.py:30
  171.2 2.2 %fusion.53 = f32[1,512]{1,0:T(1,128)S(1)} fusion(f32[512,1]{0,1:T(1,128)S(1)} %bitcast.92, f32[11,512,512]{2,1,0:T(8,128)} %get-tuple-element.241, s32[]{:T(128)} %get-tuple-element.230), kind=kOutput, calls=%fused_computation.9.clone.1 | convolution fusion | flops 3145728 | bytes 1053184 | tf_op jit(solution)/shard_map/while/body/eval_jaxpr/dot_general | solution.py:30
  173.5 2.2 %fusion.53 = f32[1,512]{1,0:T(1,128)S(1)} fusion(f32[512,1]{0,1:T(1,128)S(1)} %bitcast.92, f32[11,512,512]{2,1,0:T(8,128)} %get-tuple-element.241, s32[]{:T(128)} %get-tuple-element.230), kind=kOutput, calls=%fused_computation.9.clone.1 | convolution fusion | flops 3145728 | bytes 1053184 | tf_op jit(solution)/shard_map/while/body/eval_jaxpr/dot_general | solution.py:30
  175.9 2.2 %fusion.53 = f32[1,512]{1,0:T(1,128)S(1)} fusion(f32[512,1]{0,1:T(1,128)S(1)} %bitcast.92, f32[11,512,512]{2,1,0:T(8,128)} %get-tuple-element.241, s32[]{:T(128)} %get-tuple-element.230), kind=kOutput, calls=%fused_computation.9.clone.1 | convolution fusion | flops 3145728 | bytes 1053184 | tf_op jit(solution)/shard_map/while/body/eval_jaxpr/dot_general | solution.py:30
  178.2 2.2 %fusion.53 = f32[1,512]{1,0:T(1,128)S(1)} fusion(f32[512,1]{0,1:T(1,128)S(1)} %bitcast.92, f32[11,512,512]{2,1,0:T(8,128)} %get-tuple-element.241, s32[]{:T(128)} %get-tuple-element.230), kind=kOutput, calls=%fused_computation.9.clone.1 | convolution fusion | flops 3145728 | bytes 1053184 | tf_op jit(solution)/shard_map/while/body/eval_jaxpr/dot_general | solution.py:30
  180.6 2.2 %fusion.53 = f32[1,512]{1,0:T(1,128)S(1)} fusion(f32[512,1]{0,1:T(1,128)S(1)} %bitcast.92, f32[11,512,512]{2,1,0:T(8,128)} %get-tuple-element.241, s32[]{:T(128)} %get-tuple-element.230), kind=kOutput, calls=%fused_computation.9.clone.1 | convolution fusion | flops 3145728 | bytes 1053184 | tf_op jit(solution)/shard_map/while/body/eval_jaxpr/dot_general | solution.py:30
  182.9 2.2 %fusion.53 = f32[1,512]{1,0:T(1,128)S(1)} fusion(f32[512,1]{0,1:T(1,128)S(1)} %bitcast.92, f32[11,512,512]{2,1,0:T(8,128)} %get-tuple-element.241, s32[]{:T(128)} %get-tuple-element.230), kind=kOutput, calls=%fused_computation.9.clone.1 | convolution fusion | flops 3145728 | bytes 1053184 | tf_op jit(solution)/shard_map/while/body/eval_jaxpr/dot_general | solution.py:30
  185.3 2.2 %fusion.53 = f32[1,512]{1,0:T(1,128)S(1)} fusion(f32[512,1]{0,1:T(1,128)S(1)} %bitcast.92, f32[11,512,512]{2,1,0:T(8,128)} %get-tuple-element.241, s32[]{:T(128)} %get-tuple-element.230), kind=kOutput, calls=%fused_computation.9.clone.1 | convolution fusion | flops 3145728 | bytes 1053184 | tf_op jit(solution)/shard_map/while/body/eval_jaxpr/dot_general | solution.py:30
  (122 shorter events, 25.0 us)
Async XLA Ops:
  0.0 17.5 %copy-start.1 = (f32[12,512]{1,0:T(8,128)S(1)}, f32[12,512]{1,0:T(8,128)}, u32[]{:S(2)}) copy-start(f32[12,512]{1,0:T(8,128)} %param.8) | copy-start | bytes 73732
  0.0 17.6 %slice-start = ((f32[12,512,512]{2,1,0:T(8,128)}), f32[1,512,512]{2,1,0:T(8,128)S(1)}, s32[]{:S(2)}) async-start(f32[12,512,512]{2,1,0:T(8,128)} %param.7), calls=%async_computation.3 | async-start | bytes 2097152 | tf_op jit(solution)/shard_map/slice | solution.py:48
  0.0 17.6 %slice-start.1 = ((f32[12,512]{1,0:T(8,128)}), f32[1,512]{1,0:T(1,128)S(1)}, s32[]{:S(2)}) async-start(f32[12,512]{1,0:T(8,128)} %param.8), calls=%async_computation.4 | async-start | bytes 4096 | tf_op jit(solution)/shard_map/slice | solution.py:48
  67.1 55.9 %copy-start.3 = (u32[32]{0:T(128)S(1)}, u32[32]{0:T(128)}, u32[]{:S(2)}) copy-start(u32[32]{0:T(128)} %constant.58) | copy-start | bytes 388
  68.2 74.4 %copy-start.2 = (f32[128]{0:T(128)S(1)}, f32[128]{0:T(128)}, u32[]{:S(2)}) copy-start(f32[128]{0:T(128)} %param.9) | copy-start | bytes 1540
  68.2 17.8 %all-to-all-start = ((f32[512,4,128]{2,0,1:T(8,128)}), f32[512,4,128]{2,0,1:T(8,128)S(1)}, u32[]{:S(2)}, u32[]{:S(2)}) async-start(f32[512,4,128]{2,0,1:T(8,128)} %tile.6), calls=%async_computation | async-start | bytes 2097152 | tf_op jit(solution)/shard_map/all_to_all | solution.py:11
  72.5 13.8 %collective-permute-start = (f32[512,128]{1,0:T(8,128)S(1)}, f32[512,128]{1,0:T(8,128)S(1)}, u32[]{:S(2)}, u32[]{:S(2)}) collective-permute-start(f32[512,128]{1,0:T(8,128)S(1)} %get-tuple-element.107), channel_id=1, source_target_pairs={{0,4},{4,8},{8,12},{12,16},{16,20},{20,24},{24,28},{1,5},{5,9},{9,... | collective-permute-start | bytes 786440 | tf_op jit(solution)/shard_map/ppermute | solution.py:26
  88.1 19.4 %copy-start = (f32[512,128]{1,0:T(8,128)}, f32[512,128]{1,0:T(8,128)S(1)}, u32[]{:S(2)}) copy-start(f32[512,128]{1,0:T(8,128)S(1)} %convolution_select_fusion.2) | copy-start | bytes 786436
  89.2 17.9 %all-to-all-start.1 = ((f32[512,4,128]{2,0,1:T(8,128)}), f32[512,4,128]{2,0,1:T(8,128)S(1)}, u32[]{:S(2)}, u32[]{:S(2)}) async-start(f32[512,4,128]{2,0,1:T(8,128)} %tile.7), calls=%async_computation.1 | async-start | bytes 2097152 | tf_op jit(solution)/shard_map/all_to_all | solution.py:11
  93.7 13.8 %collective-permute-start.1 = (f32[512,128]{1,0:T(8,128)S(1)}, f32[512,128]{1,0:T(8,128)}, u32[]{:S(2)}, u32[]{:S(2)}) collective-permute-start(f32[512,128]{1,0:T(8,128)S(1)} %convolution_select_fusion.2), channel_id=1, source_target_pairs={{0,8},{4,12},{8,16},{12,20},{16,24},{20,28},{1,9},{5,13},{9,17},{1... | collective-permute-start | bytes 786440 | tf_op jit(solution)/shard_map/ppermute | solution.py:26
  95.0 20.8 %collective-permute-start.3 = (f32[512]{0:T(512)S(1)}, f32[512]{0:T(512)S(1)}, u32[]{:S(2)}, u32[]{:S(2)}) collective-permute-start(f32[512]{0:T(512)S(1)} %get-tuple-element.108), channel_id=1, source_target_pairs={{0,4},{4,8},{8,12},{12,16},{16,20},{20,24},{24,28},{1,5},{5,9},{9,... | collective-permute-start | bytes 6152 | tf_op jit(solution)/shard_map/ppermute | solution.py:26
  111.4 17.9 %all-to-all-start.2 = ((f32[512,4,128]{2,0,1:T(8,128)}), f32[512,4,128]{2,0,1:T(8,128)S(1)}, u32[]{:S(2)}, u32[]{:S(2)}) async-start(f32[512,4,128]{2,0,1:T(8,128)} %tile.8), calls=%async_computation.2 | async-start | bytes 2097152 | tf_op jit(solution)/shard_map/all_to_all | solution.py:11
  116.5 4.6 %collective-permute-start.4 = (f32[512]{0:T(512)S(1)}, f32[512]{0:T(512)S(1)}, u32[]{:S(2)}, u32[]{:S(2)}) collective-permute-start(f32[512]{0:T(512)S(1)} %add_select_fusion.2), channel_id=1, source_target_pairs={{0,8},{4,12},{8,16},{12,20},{16,24},{20,28},{1,9},{5,13},{9,17},{1... | collective-permute-start | bytes 6152 | tf_op jit(solution)/shard_map/ppermute | solution.py:26
  121.7 7.9 %collective-permute-start.5 = (f32[512]{0:T(512)S(1)}, f32[512]{0:T(512)S(1)}, u32[]{:S(2)}, u32[]{:S(2)}) collective-permute-start(f32[512]{0:T(512)S(1)} %add_select_fusion.1), channel_id=1, source_target_pairs={{0,16},{4,20},{8,24},{12,28},{1,17},{5,21},{9,25},{13,29},{2,18},{... | collective-permute-start | bytes 6152 | tf_op jit(solution)/shard_map/ppermute | solution.py:26
  124.3 16.5 %collective-permute-start.2 = (f32[512,128]{1,0:T(8,128)S(1)}, f32[512,128]{1,0:T(8,128)S(1)}, u32[]{:S(2)}, u32[]{:S(2)}) collective-permute-start(f32[512,128]{1,0:T(8,128)S(1)} %convolution_select_fusion.1), channel_id=1, source_target_pairs={{0,16},{4,20},{8,24},{12,28},{1,17},{5,21},{9,25},{13,29},{2,18},{... | collective-permute-start | bytes 786440 | tf_op jit(solution)/shard_map/ppermute | solution.py:26
  148.6 5.2 %collective-permute-start.6 = (f32[128]{0:T(128)S(1)}, f32[128]{0:T(128)S(1)}, u32[]{:S(2)}, u32[]{:S(2)}) collective-permute-start(f32[128]{0:T(128)S(1)} %dynamic-slice_add_fusion), channel_id=1, source_target_pairs={{0,4},{4,8},{8,12},{12,16},{16,20},{20,24},{24,28},{1,5},{5,9},{9,... | collective-permute-start | bytes 1544 | tf_op jit(solution)/shard_map/ppermute | solution.py:26
